TPU v7x, 256 devices: a whole 4x4x8 slice. The times are simulated.
256 devices in a mesh: gz: 4 (over y_hi, core), gy: 8 (over z), gx: 8 (over y_lo, x).
Axes of the slice: x: 4, y: 4 (y_hi: 2, y_lo: 2; y = y_hi * 2 + y_lo), z: 8, core: 2. Of those that a mesh axis runs over, the one named last changes fastest.
Arguments:
- raw_views: float32 [4, 32, 128, 1024], P(None, 'gz', 'gy', 'gx'), may hold values from 0.25 to 4
- interp_weight: float32 [4, 1024], replicated, may hold values from 0 to 1
- sample_index: int32 [4, 1024], replicated, may hold values from 0 to 1022, as said below
- psf: float32 [4, 3, 4, 9], replicated, may hold values from 0.05 to 1
- estimate: float32 [32, 128, 1024], P('gz', 'gy', 'gx'), may hold values from 0.5 to 2
Outputs:
- restored: float32 [32, 128, 1024], P('gz', 'gy', 'gx')
Inputs may be any that keep to these rules, and one draw needn't show every extreme that they name: sample_index[v, x] and sample_index[v, x] + 1 lie in the brick of 128 columns that holds column x or in one of the two bricks beside it; every view reads from a brick beside for some columns.
All inputs are finite; a program needn't handle non-finite values.
Results may differ from a plain program's by a relative error of at most 0.00005.
Values sent between devices are 32-bit elements; how exact they have to be, the bound alone decides.
A program may use at most 64 MiB of HBM per device.

v0:
```python
import jax
import jax.numpy as jnp
from jax import lax
from jax.sharding import PartitionSpec as P


def passed_along(value, axis, by):
    size = lax.axis_size(axis)
    pairs = [(i, i + by) for i in range(size) if 0 <= i + by < size]
    return lax.ppermute(value, axis, pairs)


def extended(value, sides, width):
    for axis, dim in sides:
        size, length = (lax.axis_size(axis), value.shape[dim])
        up = [(i, (i + 1) % size) for i in range(size - 1)]
        down = [(j, i) for i, j in up]
        last = lax.slice_in_dim(value, length - width, length, axis=dim)
        first = lax.slice_in_dim(value, 0, width, axis=dim)
        before = lax.ppermute(last, axis, up)
        after = lax.ppermute(first, axis, down)
        value = jnp.concatenate([before, value, after], axis=dim)
    return value


def line_pass(values, kernel, axis_num, length):
    total = kernel[0] * lax.slice_in_dim(values, 0, length, axis=axis_num)
    for tap_idx in range(1, kernel.shape[0]):
        total = total + kernel[tap_idx] * lax.slice_in_dim(
            values, tap_idx, tap_idx + length, axis=axis_num
        )
    return total


def blur_valid(padded, kernels, flipped):
    reach = kernels.shape[-1] - 1
    out_z = padded.shape[0] - reach
    out_y = padded.shape[1] - reach
    out_x = padded.shape[2] - reach
    total = None
    for rank_idx in range(kernels.shape[1]):
        kern_z = kernels[0, rank_idx]
        kern_y = kernels[1, rank_idx]
        kern_x = kernels[2, rank_idx]
        if flipped:
            kern_z = kern_z[::-1]
            kern_y = kern_y[::-1]
            kern_x = kern_x[::-1]
        result = line_pass(padded, kern_x, 2, out_x)
        result = line_pass(result, kern_y, 1, out_y)
        result = line_pass(result, kern_z, 0, out_z)
        total = result if total is None else total + result
    return total


def psf_norms(psf):
    return 1.0 / jnp.sum(jnp.prod(jnp.sum(psf, axis=-1), axis=1), axis=-1)


def resample(
    source, interp_weight, sample_index, dest_brick, src_first, src_width, columns, bricks
):
    valid = jnp.logical_and(dest_brick >= 0, dest_brick < bricks)
    start_col = jnp.clip(dest_brick, 0, bricks - 1) * columns
    firsts = lax.dynamic_slice_in_dim(sample_index, start_col, columns, 1)
    weights = lax.dynamic_slice_in_dim(interp_weight, start_col, columns, 1)
    sources = src_first + jnp.arange(src_width, dtype=jnp.int32)
    lower = firsts[:, :, None] == sources[None, None, :]
    upper = firsts[:, :, None] + 1 == sources[None, None, :]
    table = jnp.where(lower, (1.0 - weights)[:, :, None], 0.0) + jnp.where(
        upper, weights[:, :, None], 0.0
    )
    table = jnp.where(valid, table, 0.0)
    return jnp.einsum("vzys,vxs->vzyx", source, table, precision=lax.Precision.HIGHEST)


def shards(raw_views, interp_weight, sample_index, psf, estimate):
    views, planes, lines, columns = raw_views.shape
    bricks = lax.axis_size("gx")
    column_idx = lax.axis_index("gx")
    own_first = column_idx * columns
    data = resample(
        raw_views, interp_weight, sample_index, column_idx, own_first, columns, columns, bricks
    )
    for offset in (1, -1):
        contrib = resample(
            raw_views,
            interp_weight,
            sample_index,
            column_idx + offset,
            own_first,
            columns,
            columns,
            bricks,
        )
        data = data + passed_along(contrib, "gx", offset)
    half = psf.shape[-1] // 2
    norms = psf_norms(psf)
    current = estimate
    for view_idx in range(views):
        kernels = psf[view_idx]
        padded = extended(current, (("gz", 0), ("gy", 1), ("gx", 2)), half)
        blurred = blur_valid(padded, kernels, False) * norms[view_idx]
        ratio = extended(data[view_idx] / blurred, (("gz", 0), ("gy", 1), ("gx", 2)), half)
        current = current * (blur_valid(ratio, kernels, True) * norms[view_idx])
    return current


def solution(mesh):
    return jax.shard_map(
        shards,
        mesh=mesh,
        in_specs=(P(None, "gz", "gy", "gx"), P(), P(), P(), P("gz", "gy", "gx")),
        out_specs=P("gz", "gy", "gx"),
        check_vma=False,
    )
```

profile of v0, /device:TPU:1, one launch (start us, length us, event | category | flops | bytes accessed | tf_op | source)
XLA Modules:
  0.0 820.0 jit_solution(2742653098763299305)
XLA Ops:
  41.0 6.0 multiply_add_fusion.30
  52.8 6.1 multiply_add_fusion.29
  64.6 6.0 multiply_add_fusion.28
  88.9 23.4 %fusion.562 = f32[8,16,128]{2,1,0:T(8,128)S(1)} fusion(f32[16,16,128]{2,1,0:T(8,128)S(1)} %fusion.247, f32[16,16,128]{2,1,0:T(8,128)S(1)} %fusion.255, f32[16,16,128]{2,1,0:T(8,128)S(1)} %fusion.263, f32[16,16,128]{2,1,0:T(8,128)S(1)} %fusion.271, f32[4,8,16,128]{3,2,1,0:T(8,128)S(1)} %fusion.1, f32[]{:T(128)} %bitcast.119, f32[]{:T(128)} %bitcast.118, ...), kind=kLoop, calls=%fused_computation.1165 | loop fusion | flops 1196032 | bytes 2490516 | tf_op jit(solution)/shard_map/div | solution.py:104
  112.3 6.5 collective-permute-start.8
  169.2 6.1 multiply_add_fusion.25
  180.9 6.0 multiply_add_fusion.24
  192.7 23.4 %fusion.525 = f32[8,16,128]{2,1,0:T(8,128)S(1)} fusion(f32[8,16,128]{2,1,0:T(8,128)S(1)} %copy-done.1, f32[16,16,128]{2,1,0:T(8,128)S(1)} %fusion.215, f32[16,16,128]{2,1,0:T(8,128)S(1)} %fusion.223, f32[16,16,128]{2,1,0:T(8,128)S(1)} %fusion.231, f32[16,16,128]{2,1,0:T(8,128)S(1)} %fusion.239, f32[]{:T(128)} %bitcast.119, f32[]{:T(128)} %bitcast.118, ...), kind=kLoop, calls=%fused_computation.1092 | loop fusion | flops 1196032 | bytes 2490516 | tf_op jit(solution)/shard_map/mul | solution.py:105
  249.7 6.0 multiply_add_fusion.23
  272.9 6.1 multiply_add_fusion.21
  296.2 23.2 %fusion.488 = f32[8,16,128]{2,1,0:T(8,128)S(1)} fusion(f32[16,16,128]{2,1,0:T(8,128)S(1)} %fusion.183, f32[16,16,128]{2,1,0:T(8,128)S(1)} %fusion.191, f32[16,16,128]{2,1,0:T(8,128)S(1)} %fusion.199, f32[16,16,128]{2,1,0:T(8,128)S(1)} %fusion.207, f32[4,8,16,128]{3,2,1,0:T(8,128)S(1)} %fusion.1, f32[]{:T(128)} %bitcast.230, f32[]{:T(128)} %bitcast.229, ...), kind=kLoop, calls=%fused_computation.1018 | loop fusion | flops 1196032 | bytes 2490516 | tf_op jit(solution)/shard_map/div | solution.py:104
  349.8 6.0 multiply_add_fusion.19
  373.0 6.1 multiply_add_fusion.17
  396.3 23.2 %fusion.451 = f32[8,16,128]{2,1,0:T(8,128)S(1)} fusion(f32[8,16,128]{2,1,0:T(8,128)S(1)} %fusion.525, f32[16,16,128]{2,1,0:T(8,128)S(1)} %fusion.151, f32[16,16,128]{2,1,0:T(8,128)S(1)} %fusion.159, f32[16,16,128]{2,1,0:T(8,128)S(1)} %fusion.167, f32[16,16,128]{2,1,0:T(8,128)S(1)} %fusion.175, f32[]{:T(128)} %bitcast.230, f32[]{:T(128)} %bitcast.229, ...), kind=kLoop, calls=%fused_computation.945 | loop fusion | flops 1196032 | bytes 2490516 | tf_op jit(solution)/shard_map/mul | solution.py:105
  449.2 6.0 multiply_add_fusion.15
  460.8 6.2 multiply_add_fusion.14
  472.6 6.0 multiply_add_fusion.13
  484.3 6.2 multiply_add_fusion.12
  496.4 23.1 %fusion.414 = f32[8,16,128]{2,1,0:T(8,128)S(1)} fusion(f32[16,16,128]{2,1,0:T(8,128)S(1)} %fusion.119, f32[16,16,128]{2,1,0:T(8,128)S(1)} %fusion.127, f32[16,16,128]{2,1,0:T(8,128)S(1)} %fusion.135, f32[16,16,128]{2,1,0:T(8,128)S(1)} %fusion.143, f32[4,8,16,128]{3,2,1,0:T(8,128)S(1)} %fusion.1, f32[]{:T(128)} %bitcast.341, f32[]{:T(128)} %bitcast.340, ...), kind=kLoop, calls=%fused_computation.871 | loop fusion | flops 1196032 | bytes 2490516 | tf_op jit(solution)/shard_map/div | solution.py:104
  549.1 6.0 multiply_add_fusion.11
  560.8 6.2 multiply_add_fusion.10
  572.6 6.0 multiply_add_fusion.9
  584.3 6.2 multiply_add_fusion.8
  596.3 23.1 %fusion.377 = f32[8,16,128]{2,1,0:T(8,128)S(1)} fusion(f32[8,16,128]{2,1,0:T(8,128)S(1)} %fusion.451, f32[16,16,128]{2,1,0:T(8,128)S(1)} %fusion.87, f32[16,16,128]{2,1,0:T(8,128)S(1)} %fusion.95, f32[16,16,128]{2,1,0:T(8,128)S(1)} %fusion.103, f32[16,16,128]{2,1,0:T(8,128)S(1)} %fusion.111, f32[]{:T(128)} %bitcast.341, f32[]{:T(128)} %bitcast.340, ...), kind=kLoop, calls=%fused_computation.798 | loop fusion | flops 1196032 | bytes 2490516 | tf_op jit(solution)/shard_map/mul | solution.py:105
  649.1 6.2 multiply_add_fusion.7
  672.9 6.0 multiply_add_fusion.5
  684.7 6.0 multiply_add_fusion.4
  696.3 23.1 %fusion.340 = f32[8,16,128]{2,1,0:T(8,128)S(1)} fusion(f32[16,16,128]{2,1,0:T(8,128)S(1)} %fusion.55, f32[16,16,128]{2,1,0:T(8,128)S(1)} %fusion.63, f32[16,16,128]{2,1,0:T(8,128)S(1)} %fusion.71, f32[16,16,128]{2,1,0:T(8,128)S(1)} %fusion.79, f32[4,8,16,128]{3,2,1,0:T(8,128)S(1)} %fusion.1, f32[]{:T(128)} %bitcast.452, f32[]{:T(128)} %bitcast.451, ...), kind=kLoop, calls=%fused_computation.724 | loop fusion | flops 1196032 | bytes 2490516 | tf_op jit(solution)/shard_map/div | solution.py:104
  749.1 6.2 multiply_add_fusion.3
  772.9 6.0 multiply_add_fusion.1
  784.6 6.0 multiply_add_fusion
  796.3 23.7 %fusion.303 = f32[8,16,128]{2,1,0:T(8,128)} fusion(f32[8,16,128]{2,1,0:T(8,128)S(1)} %fusion.377, f32[16,16,128]{2,1,0:T(8,128)S(1)} %fusion.23, f32[16,16,128]{2,1,0:T(8,128)S(1)} %fusion.31, f32[16,16,128]{2,1,0:T(8,128)S(1)} %fusion.39, f32[16,16,128]{2,1,0:T(8,128)S(1)} %fusion.47, f32[]{:T(128)} %bitcast.452, f32[]{:T(128)} %bitcast.451, f32[]{:T(128)} %bitcast.450, ...), kind=kLoop, calls=%fused_computation.651 | loop fusion | flops 1196032 | bytes 2490516 | tf_op jit(solution)/shard_map/mul | solution.py:105
  (225 shorter events, 486.8 us)
Async XLA Ops:
  2.5 85.5 %collective-permute-start = (f32[4,8,16,128]{3,2,1,0:T(8,128)S(1)}, f32[4,8,16,128]{3,2,1,0:T(8,128)S(1)}, u32[]{:S(2)}, u32[]{:S(2)}) collective-permute-start(f32[4,8,16,128]{3,2,1,0:T(8,128)S(1)} %convolution_bitcast_fusion.1), channel_id=1, source_target_pairs={{0,1},{1,2},{2,3},{3,4},{4,5},{5,6},{6,7},{8,9},{9,10},{10,11},{11... | collective-permute-start | bytes 786440 | tf_op jit(solution)/shard_map/ppermute | solution.py:10
  7.3 80.6 %collective-permute-start.1 = (f32[4,8,16,128]{3,2,1,0:T(8,128)S(1)}, f32[4,8,16,128]{3,2,1,0:T(8,128)S(1)}, u32[]{:S(2)}, u32[]{:S(2)}) collective-permute-start(f32[4,8,16,128]{3,2,1,0:T(8,128)S(1)} %convolution_bitcast_fusion), channel_id=1, source_target_pairs={{1,0},{2,1},{3,2},{4,3},{5,4},{6,5},{7,6},{9,8},{10,9},{11,10},{12... | collective-permute-start | bytes 786440 | tf_op jit(solution)/shard_map/ppermute | solution.py:10
  8.7 11.5 %collective-permute-start.2 = (f32[4,16,128]{2,1,0:T(8,128)S(1)}, f32[4,16,128]{2,1,0:T(8,128)S(1)}, u32[]{:S(2)}, u32[]{:S(2)}) collective-permute-start(f32[4,16,128]{2,1,0:T(8,128)S(1)} %get-tuple-element.80), channel_id=1, source_target_pairs={{0,64},{64,128},{128,192},{1,65},{65,129},{129,193},{2,66},{66,130... | collective-permute-start | bytes 98312 | tf_op jit(solution)/shard_map/ppermute | solution.py:20
  14.3 6.7 collective-permute-start.3
  29.6 7.1 collective-permute-start.6
  33.9 6.9 collective-permute-start.7
  112.3 9.2 %collective-permute-start.8 = (f32[4,16,128]{2,1,0:T(8,128)S(1)}, f32[4,16,128]{2,1,0:T(8,128)S(1)}, u32[]{:S(2)}, u32[]{:S(2)}) collective-permute-start(f32[4,16,128]{2,1,0:T(8,128)S(1)} %get-tuple-element.77), channel_id=1, source_target_pairs={{0,64},{64,128},{128,192},{1,65},{65,129},{129,193},{2,66},{66,130... | collective-permute-start | bytes 98312 | tf_op jit(solution)/shard_map/ppermute | solution.py:20
  118.8 6.7 collective-permute-start.9
  138.3 7.2 collective-permute-start.13
  216.1 6.8 collective-permute-start.14
  220.2 6.7 collective-permute-start.15
  227.0 6.9 collective-permute-start.16
  236.9 8.4 %collective-permute-start.18 = (f32[16,24,4]{2,1,0:T(8,128)S(1)}, f32[16,24,4]{2,1,0:T(8,128)S(1)}, u32[]{:S(2)}, u32[]{:S(2)}) collective-permute-start(f32[16,24,4]{2,1,0:T(8,128)S(1)} %get-tuple-element.39), channel_id=1, source_target_pairs={{0,1},{1,2},{2,3},{3,4},{4,5},{5,6},{6,7},{8,9},{9,10},{10,11},{11... | collective-permute-start | bytes 18440 | tf_op jit(solution)/shard_map/ppermute | solution.py:20
  242.7 6.8 collective-permute-start.19
  319.4 6.8 collective-permute-start.20
  323.6 6.7 collective-permute-start.21
  338.8 6.7 collective-permute-start.24
  342.5 7.1 collective-permute-start.25
  419.5 6.8 collective-permute-start.26
  423.7 6.7 collective-permute-start.27
  438.1 6.7 collective-permute-start.30
  441.9 7.1 collective-permute-start.31
  519.5 6.8 collective-permute-start.32
  523.6 6.7 collective-permute-start.33
  538.1 6.7 collective-permute-start.36
  541.8 7.1 collective-permute-start.37
  619.5 6.8 collective-permute-start.38
  623.6 6.7 collective-permute-start.39
  638.0 6.7 collective-permute-start.42
  641.8 7.1 collective-permute-start.43
  723.6 6.7 collective-permute-start.45
  741.7 7.1 collective-permute-start.49
  (21 other events, 106.0 us)
where the time goes:
time: 830 us; the launch traced here: 820 us
  other arithmetic  565 us (68%)
  starting transfers between devices  137 us (17%)
  waiting for transfers between devices  94.2 us (11%)
  local copies, waits for them, and re-layouts  18.9 us (2%)
    add x64, other arithmetic, line_pass(): total + kernel[tap_idx] * lax.slice_in_dim(values, tap_idx, tap_idx + len...  375 us
    ppermute x24, starting transfers between devices, extended(): before = lax.ppermute(last, axis, up)  95.8 us
    mul x4, other arithmetic, shards(): current = current * (blur_valid(ratio, kernels, True) * norms[view_idx])  93.5 us
    div x4, other arithmetic, shards(): data[view_idx] / blurred  92.9 us
    ppermute x24, waiting for transfers between devices, extended(): after = lax.ppermute(first, axis, down)  87 us
    ppermute x24, starting transfers between devices, extended(): after = lax.ppermute(first, axis, down)  36.4 us
  transfers between devices with their start and end apart: 50, of which 32 were waited for; matrix products, arithmetic and copies ran while one was open for 8% of the time, Pallas kernels for 0%

commit v1 on v0

v1 whole, which is shorter than its diff:
```python
import jax
import jax.numpy as jnp
from jax import lax
from jax.experimental import pallas as pl
from jax.experimental.pallas import tpu as pltpu
from jax.sharding import PartitionSpec as P

MESH = pl.DeviceIdType.MESH
F32 = jnp.float32
STEPS = (-1, 0, 1)
AROUND = [(dz, dy, dx) for dx in STEPS for dz in STEPS for dy in STEPS if (dz, dy, dx) != (0, 0, 0)]
HALF = 4
TAPS = 9
RANK = 4


def window(ref, slot, dz, dy, arriving):
    planes = {
        0: (4, 8),
        1: (12, 4) if arriving else (8, 4),
        -1: (0, 4) if arriving else (4, 4),
    }[dz]
    rows = {
        0: (8, 16),
        1: (24, 8) if arriving else (16, 8),
        -1: (0, 8) if arriving else (8, 8),
    }[dy]
    return ref.at[slot, pl.ds(*planes), pl.ds(*rows), :]


def kernel(
    sizes,
    psf_ref,
    weight_ref,
    index_ref,
    raw_ref,
    est_ref,
    out_ref,
    field,
    edge_out,
    edge_in,
    mixed,
    after_x,
    after_z,
    beside,
    data,
    send_sem,
    recv_sem,
    raw_send,
    raw_recv,
):
    views = raw_ref.shape[0]
    spots = [lax.axis_index(a) for a in ("gz", "gy", "gx")]
    here = dict(zip(("gz", "gy", "gx"), spots))

    def peer(dz, dy, dx):
        spot = {}
        for axis, by in (("gz", dz), ("gy", dy), ("gx", dx)):
            spot[axis] = lax.rem(here[axis] + (by + sizes[axis]), sizes[axis])
        return spot

    barrier = pltpu.get_barrier_semaphore()
    for offset in AROUND:
        pl.semaphore_signal(barrier, inc=1, device_id=peer(*offset), device_id_type=MESH)

    lane8 = lax.broadcasted_iota(jnp.int32, (8, 128), 1)
    sub8 = lax.broadcasted_iota(jnp.int32, (8, 128), 0)
    lane16 = lax.broadcasted_iota(jnp.int32, (16, 128), 1)
    lane24 = lax.broadcasted_iota(jnp.int32, (24, 128), 1)
    inside = {}
    for axis in ("gz", "gy", "gx"):
        inside[axis] = (
            (here[axis] > 0).astype(jnp.int32),
            (here[axis] < sizes[axis] - 1).astype(jnp.int32),
        )
    from_right8 = (lane8 % 8) >= 4
    rows_ok = jnp.where(sub8 < 4, inside["gy"][1], inside["gy"][0])
    cols_ok = jnp.where(from_right8, inside["gx"][1], inside["gx"][0])

    def packed(pack, plane, num):
        moved = pltpu.roll(plane, 4 + 8 * num, 1)
        return jnp.where(lane16 // 8 == num, moved, pack)

    def halo_copies(slot):
        copies = []
        for num, (dz, dy, dx) in enumerate(AROUND):
            if dx == 0:
                src = window(field, slot, dz, dy, False)
                dst = window(field, slot, -dz, -dy, True)
            else:
                src = edge_out.at[slot]
                dst = edge_in.at[slot, (1 - dx) // 2, 1 - dz, 1 - dy]
            copies.append(
                pltpu.make_async_remote_copy(
                    src_ref=src,
                    dst_ref=dst,
                    send_sem=send_sem.at[slot, num],
                    recv_sem=recv_sem.at[slot, num],
                    device_id=peer(dz, dy, dx),
                    device_id_type=MESH,
                )
            )
        return copies

    def raw_copies(view):
        return [
            pltpu.make_async_remote_copy(
                src_ref=raw_ref.at[view],
                dst_ref=beside.at[side, view],
                send_sem=raw_send.at[side, view],
                recv_sem=raw_recv.at[side, view],
                device_id=peer(0, 0, by),
                device_id_type=MESH,
            )
            for side, by in ((0, 1), (1, -1))
        ]

    def make_data(view):
        for copy in raw_copies(view):
            copy.wait()
        own = pl.ds(pl.multiple_of(here["gx"] * 128, 128), 128)
        row = lax.broadcasted_iota(jnp.int32, (views, 128), 0)
        first = jnp.sum(jnp.where(row == view, index_ref[:, own], 0), axis=0, keepdims=True)
        weight = jnp.sum(jnp.where(row == view, weight_ref[:, own], 0.0), axis=0, keepdims=True)
        source = lax.broadcasted_iota(jnp.int32, (128, 128), 0)
        total = None
        for brick, ref in ((-1, beside.at[0]), (0, raw_ref), (1, beside.at[1])):
            at = source + (here["gx"] + brick) * 128
            table = jnp.where(at == first, 1.0 - weight, 0.0)
            table = table + jnp.where(at == first + 1, weight, 0.0)
            part = jnp.dot(
                ref[view].reshape(128, 128),
                table,
                precision=lax.Precision.HIGHEST,
                preferred_element_type=F32,
            )
            total = part if total is None else total + part
        data[...] = total.reshape(8, 16, 128)

    def taps(view, axis, flipped):
        return [
            [psf_ref[view, axis, r, TAPS - 1 - t if flipped else t] for t in range(TAPS)]
            for r in range(RANK)
        ]

    def norm_of(view):
        total = 0.0
        for r in range(RANK):
            prod = None
            for axis in range(3):
                line = psf_ref[view, axis, r, 0]
                for t in range(1, TAPS):
                    line = line + psf_ref[view, axis, r, t]
                prod = line if prod is None else prod * line
            total = total + prod
        return 1.0 / jnp.full((16, 128), total, F32)

    def blur(slot, view, flipped, use):
        kx = taps(view, 2, flipped)
        for dz in range(3):
            seen = []
            for dy in range(3):
                left, right = edge_in[slot, 0, dz, dy], edge_in[slot, 1, dz, dy]
                both = jnp.where((lane16 % 8) >= 4, right, left)
                cols16 = jnp.concatenate([cols_ok, cols_ok], axis=0)
                seen.append(jnp.where(cols16 > 0, both, 0.0))
            ok = jnp.full((8, 128), (inside["gz"][0], 1, inside["gz"][1])[dz], jnp.int32)
            ok16 = jnp.concatenate([ok, ok], axis=0)
            edge = jnp.where(sub8 < 4, seen[2][0:8], seen[0][8:16])
            mixed[dz, 0:8] = jnp.where(jnp.logical_and(rows_ok > 0, ok > 0), edge, 0.0)
            mixed[dz, 8:24] = jnp.where(ok16 > 0, seen[1], 0.0)

        def x_step(i, carry):
            part = (i + 1) // 2
            ok = jnp.where(i == 0, inside["gz"][0], jnp.where(i == 3, inside["gz"][1], 1))
            ok8 = jnp.full((8, 128), ok, jnp.int32)
            ok16 = jnp.full((16, 128), ok, jnp.int32)
            halo = mixed[part]
            for j in range(4):
                z = i * 4 + j
                edge = jnp.where(sub8 < 4, field[slot, z, 24:32], field[slot, z, 0:8])
                edge = jnp.where(jnp.logical_and(rows_ok > 0, ok8 > 0), edge, 0.0)
                own = jnp.where(ok16 > 0, field[slot, z, 8:24], 0.0)
                here_f = jnp.concatenate([edge, own], axis=0)
                shift = 128 - 4 - 8 * j - 32 * ((i + 1) % 2)
                side = pltpu.roll(halo, shift, 1)
                sums = [None] * RANK
                for t in range(TAPS):
                    s = t - HALF
                    if s == 0:
                        moved = here_f
                    elif s > 0:
                        moved = pltpu.roll(jnp.where(lane24 < s, side, here_f), 128 - s, 1)
                    else:
                        moved = pltpu.roll(jnp.where(lane24 >= 128 + s, side, here_f), -s, 1)
                    for r in range(RANK):
                        term = kx[r][t] * moved
                        sums[r] = term if sums[r] is None else sums[r] + term
                for r in range(RANK):
                    after_x[r, z] = sums[r]
            return carry

        lax.fori_loop(0, 4, x_step, 0)
        kz = taps(view, 0, flipped)

        def z_step(z, carry):
            for r in range(RANK):
                total = kz[r][0] * after_x[r, z]
                for t in range(1, TAPS):
                    total = total + kz[r][t] * after_x[r, z + t]
                after_z[r, z, 0:24] = total
                after_z[r, z, 24:32] = total[0:8]
            return carry

        lax.fori_loop(0, 8, z_step, 0)
        ky = taps(view, 1, flipped)

        def y_step(z, pack):
            total = None
            for r in range(RANK):
                for t in range(TAPS):
                    term = ky[r][t] * after_z[r, z, HALF + t : HALF + t + 16]
                    total = term if total is None else total + term
            plane = use(z, total)
            return packed(pack, plane, z)

        return lax.fori_loop(0, 8, y_step, jnp.zeros((16, 128), F32))

    pack = jnp.zeros((16, 128), F32)
    for z in range(8):
        plane = est_ref[z]
        field[0, 4 + z, 8:24] = plane
        pack = packed(pack, plane, z)
    edge_out[0] = pack

    pl.semaphore_wait(barrier, len(AROUND))

    for copy in halo_copies(0):
        copy.start()
    for view in range(views):
        for copy in raw_copies(view):
            copy.start()

    def view_step(view, carry):
        make_data(view)
        norm = norm_of(view)
        for copy in halo_copies(0):
            copy.wait()

        def to_ratio(z, total):
            plane = data[z] / (total * norm)
            field[1, 4 + z, 8:24] = plane
            return plane

        edge_out[1] = blur(0, view, False, to_ratio)
        for copy in halo_copies(1):
            copy.start()
        for copy in halo_copies(1):
            copy.wait()

        def to_current(z, total):
            plane = field[0, 4 + z, 8:24] * (total * norm)
            field[0, 4 + z, 8:24] = plane
            out_ref[z] = plane
            return plane

        edge_out[0] = blur(1, view, True, to_current)

        @pl.when(view < views - 1)
        def _():
            for copy in halo_copies(0):
                copy.start()

        return carry

    lax.fori_loop(0, views, view_step, 0)


def solution(mesh):
    sizes = dict(mesh.shape)

    def shards(raw_views, interp_weight, sample_index, psf, estimate):
        vmem = pl.BlockSpec(memory_space=pltpu.VMEM)
        smem = pl.BlockSpec(memory_space=pltpu.SMEM)
        num = len(AROUND)
        views = raw_views.shape[0]

        def body(*refs):
            kernel(sizes, *refs)

        return pl.pallas_call(
            body,
            out_shape=jax.ShapeDtypeStruct(estimate.shape, F32),
            in_specs=[smem, vmem, vmem, vmem, vmem],
            out_specs=vmem,
            scratch_shapes=[
                pltpu.VMEM((2, 16, 32, 128), F32),
                pltpu.VMEM((2, 16, 128), F32),
                pltpu.VMEM((2, 2, 3, 3, 16, 128), F32),
                pltpu.VMEM((3, 24, 128), F32),
                pltpu.VMEM((RANK, 16, 24, 128), F32),
                pltpu.VMEM((RANK, 8, 32, 128), F32),
                pltpu.VMEM((2, views, 8, 16, 128), F32),
                pltpu.VMEM((8, 16, 128), F32),
                pltpu.SemaphoreType.DMA((2, num)),
                pltpu.SemaphoreType.DMA((2, num)),
                pltpu.SemaphoreType.DMA((2, views)),
                pltpu.SemaphoreType.DMA((2, views)),
            ],
            compiler_params=pltpu.CompilerParams(collective_id=0, has_side_effects=True),
            name="deconvolve",
        )(psf, interp_weight, sample_index, raw_views, estimate)

    return jax.shard_map(
        shards,
        mesh=mesh,
        in_specs=(P(None, "gz", "gy", "gx"), P(), P(), P(), P("gz", "gy", "gx")),
        out_specs=P("gz", "gy", "gx"),
        check_vma=False,
    )
```

time: 830 us -> 87.7 us (0.11); the launches traced: 820 us -> 87.5 us
  other arithmetic: 565 us -> 0 us
  starting transfers between devices: 137 us -> 0 us
  waiting for transfers between devices: 94.2 us -> 0 us
  Pallas kernels: 0 us -> 86 us
  local copies, waits for them, and re-layouts: 18.9 us -> 1.47 us
    add x66 -> x0, other arithmetic: 376 us -> none  [the longest x64 375 us: line_pass(): total + kernel[tap_idx] * lax.slice_in_dim(values, tap_idx, tap_idx + len...]
    ppermute x50 -> x0, starting transfers between devices: 137 us -> none  [the longest x24 95.8 us: extended(): before = lax.ppermute(last, axis, up)]
    ppermute x50 -> x0, waiting for transfers between devices: 94.2 us -> none  [the longest x24 87 us: extended(): after = lax.ppermute(first, axis, down)]
    mul x4 -> x0, other arithmetic: 93.5 us -> none  [shards(): current = current * (blur_valid(ratio, kernels, True) * norms[view_idx])]
    div x5 -> x0, other arithmetic: 92.9 us -> none  [the longest x4 92.9 us: shards(): data[view_idx] / blurred]
    pallas_call x0 -> x1, Pallas kernels: none -> 86 us  [shards(): pl.pallas_call(body, out_shape=jax.ShapeDtypeStruct(estimate.shape, F32),...]
    slice x42 -> x0, local copies, waits for them, and re-layouts: 18.9 us -> none  [the longest x12 8.72 us: line_pass(): kernel[tap_idx]]
  transfers between devices with their start and end apart: 50 -> 0, of which waited for: 32 -> 0; matrix products, arithmetic and copies ran while one was open for 8% -> 0% of each run, Pallas kernels for 0% -> 0%
where the time goes in v1:
time: 87.7 us; the launch traced here: 87.5 us
  Pallas kernels  86 us (98%)
  local copies, waits for them, and re-layouts  1.47 us (2%)
    pallas_call x1, Pallas kernels, shards(): pl.pallas_call(body, out_shape=jax.ShapeDtypeStruct(estimate.shape, F32),...  86 us

profile of v1, /device:TPU:1, one launch (start us, length us, event | category | flops | bytes accessed | tf_op | source)
XLA Modules:
  0.0 87.5 jit_solution(16774226827508313731)
XLA Ops:
  0.0 86.0 %deconvolve.1 = f32[8,16,128]{2,1,0:T(8,128)} custom-call(f32[4,3,4,9]{3,2,1,0:T(4,128)} %refs_0_.1, f32[4,1024]{1,0:T(4,128)} %refs_1_.1, s32[4,1024]{1,0:T(4,128)} %refs_2_.1, f32[4,8,16,128]{3,2,1,0:T(8,128)} %refs_3_.1, f32[8,16,128]{2,1,0:T(8,128)} %refs_4_.1), custom_call_target="tpu_custom_call" | custom-call | tf_op jit(solution)/shard_map/deconvolve/pallas_call | solution.py:291
  86.0 1.5 %copy.7 = f32[8,16,128]{2,1,0:T(8,128)} copy(f32[8,16,128]{2,1,0:T(8,128)} %deconvolve.1) | data formatting | bytes 131072

commit v2 on v1

--- a/solution.py
+++ b/solution.py
@@ -22,8 +22,8 @@
     }[dz]
     rows = {
         0: (8, 16),
-        1: (24, 8) if arriving else (16, 8),
-        -1: (0, 8) if arriving else (8, 8),
+        1: (24, 4) if arriving else (20, 4),
+        -1: (4, 4) if arriving else (8, 4),
     }[dy]
     return ref.at[slot, pl.ds(*planes), pl.ds(*rows), :]
 
@@ -88,8 +88,9 @@
                 src = window(field, slot, dz, dy, False)
                 dst = window(field, slot, -dz, -dy, True)
             else:
-                src = edge_out.at[slot]
-                dst = edge_in.at[slot, (1 - dx) // 2, 1 - dz, 1 - dy]
+                rows = pl.ds(*{0: (0, 16), 1: (12, 4), -1: (0, 4)}[dy])
+                src = edge_out.at[slot, rows]
+                dst = edge_in.at[slot, (1 - dx) // 2, 1 - dz, 1 - dy, rows]
             copies.append(
                 pltpu.make_async_remote_copy(
                     src_ref=src,

time: 87.7 us -> 79.8 us (0.910)
  Pallas kernels: 86 us -> 78.2 us
    pallas_call x1, Pallas kernels: 86 us -> 78.2 us  [shards(): pl.pallas_call(body, out_shape=jax.ShapeDtypeStruct(estimate.shape, F32),...]
where the time goes in v2:
time: 79.8 us; the launch traced here: 79.6 us
  Pallas kernels  78.2 us (98%)
  local copies, waits for them, and re-layouts  1.47 us (2%)
    pallas_call x1, Pallas kernels, shards(): pl.pallas_call(body, out_shape=jax.ShapeDtypeStruct(estimate.shape, F32),...  78.2 us

profile of v2, /device:TPU:1, one launch (start us, length us, event | category | flops | bytes accessed | tf_op | source)
XLA Modules:
  0.0 79.6 jit_solution(11619348815507663806)
XLA Ops:
  0.0 78.2 %deconvolve.1 = f32[8,16,128]{2,1,0:T(8,128)} custom-call(f32[4,3,4,9]{3,2,1,0:T(4,128)} %refs_0_.1, f32[4,1024]{1,0:T(4,128)} %refs_1_.1, s32[4,1024]{1,0:T(4,128)} %refs_2_.1, f32[4,8,16,128]{3,2,1,0:T(8,128)} %refs_3_.1, f32[8,16,128]{2,1,0:T(8,128)} %refs_4_.1), custom_call_target="tpu_custom_call" | custom-call | tf_op jit(solution)/shard_map/deconvolve/pallas_call | solution.py:292
  78.2 1.5 %copy.7 = f32[8,16,128]{2,1,0:T(8,128)} copy(f32[8,16,128]{2,1,0:T(8,128)} %deconvolve.1) | data formatting | bytes 131072

commit v3 on v2

--- a/solution.py
+++ b/solution.py
@@ -39,7 +39,7 @@
     field,
     edge_out,
     edge_in,
-    mixed,
+    part,
     after_x,
     after_z,
     beside,
@@ -81,9 +81,10 @@
         moved = pltpu.roll(plane, 4 + 8 * num, 1)
         return jnp.where(lane16 // 8 == num, moved, pack)
 
-    def halo_copies(slot):
-        copies = []
-        for num, (dz, dy, dx) in enumerate(AROUND):
+    peers = {offset: peer(*offset) for offset in AROUND}
+
+    def send_halos(slot):
+        for dz, dy, dx in AROUND:
             if dx == 0:
                 src = window(field, slot, dz, dy, False)
                 dst = window(field, slot, -dz, -dy, True)
@@ -91,17 +92,19 @@
                 rows = pl.ds(*{0: (0, 16), 1: (12, 4), -1: (0, 4)}[dy])
                 src = edge_out.at[slot, rows]
                 dst = edge_in.at[slot, (1 - dx) // 2, 1 - dz, 1 - dy, rows]
-            copies.append(
-                pltpu.make_async_remote_copy(
-                    src_ref=src,
-                    dst_ref=dst,
-                    send_sem=send_sem.at[slot, num],
-                    recv_sem=recv_sem.at[slot, num],
-                    device_id=peer(dz, dy, dx),
-                    device_id_type=MESH,
-                )
-            )
-        return copies
+            kind = 0 if dx == 0 else 1
+            pltpu.make_async_remote_copy(
+                src_ref=src,
+                dst_ref=dst,
+                send_sem=send_sem.at[slot, kind],
+                recv_sem=recv_sem.at[slot, kind],
+                device_id=peers[dz, dy, dx],
+                device_id_type=MESH,
+            ).start()
+
+    def wait_halos(slot, kind, sem):
+        whole = field.at[slot, :, pl.ds(0, 16), :] if kind == 0 else edge_in.at[slot, 0]
+        pltpu.make_async_copy(whole, whole, sem.at[slot, kind]).wait()
 
     def raw_copies(view):
         return [
@@ -156,53 +159,81 @@
             total = total + prod
         return 1.0 / jnp.full((16, 128), total, F32)
 
-    def blur(slot, view, flipped, use):
-        kx = taps(view, 2, flipped)
-        for dz in range(3):
-            seen = []
-            for dy in range(3):
-                left, right = edge_in[slot, 0, dz, dy], edge_in[slot, 1, dz, dy]
-                both = jnp.where((lane16 % 8) >= 4, right, left)
-                cols16 = jnp.concatenate([cols_ok, cols_ok], axis=0)
-                seen.append(jnp.where(cols16 > 0, both, 0.0))
-            ok = jnp.full((8, 128), (inside["gz"][0], 1, inside["gz"][1])[dz], jnp.int32)
-            ok16 = jnp.concatenate([ok, ok], axis=0)
-            edge = jnp.where(sub8 < 4, seen[2][0:8], seen[0][8:16])
-            mixed[dz, 0:8] = jnp.where(jnp.logical_and(rows_ok > 0, ok > 0), edge, 0.0)
-            mixed[dz, 8:24] = jnp.where(ok16 > 0, seen[1], 0.0)
-
-        def x_step(i, carry):
-            part = (i + 1) // 2
-            ok = jnp.where(i == 0, inside["gz"][0], jnp.where(i == 3, inside["gz"][1], 1))
+    def x_lines(lines, kx, store):
+        lane = lax.broadcasted_iota(jnp.int32, lines.shape, 1)
+        sums = [None] * RANK
+        for t in range(TAPS):
+            s = t - HALF
+            if s == 0:
+                moved = lines
+            elif s > 0:
+                moved = pltpu.roll(jnp.where(lane < s, 0.0, lines), 128 - s, 1)
+            else:
+                moved = pltpu.roll(jnp.where(lane >= 128 + s, 0.0, lines), -s, 1)
+            for r in range(RANK):
+                term = kx[r][t] * moved
+                sums[r] = term if sums[r] is None else sums[r] + term
+        for r in range(RANK):
+            store(r, sums[r])
+
+    def y_lines(ky, z):
+        total = None
+        for r in range(RANK):
+            for t in range(TAPS):
+                term = ky[r][t] * after_z[r, z, HALF + t : HALF + t + 16]
+                total = term if total is None else total + term
+        return total
+
+    def edge_rows(slot, z, ok):
+        edge = jnp.where(sub8 < 4, field[slot, z, 24:32], field[slot, z, 0:8])
+        return jnp.where(jnp.logical_and(rows_ok > 0, ok > 0), edge, 0.0)
+
+    def blur(slot, view, flipped, use, meanwhile):
+        kz, ky, kx = [taps(view, axis, flipped) for axis in range(3)]
+
+        def own_step(i, carry):
+            for j in range(4):
+                z = 4 + i * 4 + j
+
+                def store(r, value):
+                    after_x[r, z, 8:24] = value
+
+                x_lines(field[slot, z, 8:24], kx, store)
+            return carry
+
+        lax.fori_loop(0, 2, own_step, 0)
+        meanwhile()
+        wait_halos(slot, 0, recv_sem)
+
+        def far_step(i, carry):
+            ok = jnp.where(i == 0, inside["gz"][0], inside["gz"][1])
             ok8 = jnp.full((8, 128), ok, jnp.int32)
             ok16 = jnp.full((16, 128), ok, jnp.int32)
-            halo = mixed[part]
             for j in range(4):
-                z = i * 4 + j
-                edge = jnp.where(sub8 < 4, field[slot, z, 24:32], field[slot, z, 0:8])
-                edge = jnp.where(jnp.logical_and(rows_ok > 0, ok8 > 0), edge, 0.0)
+                z = 12 * i + j
                 own = jnp.where(ok16 > 0, field[slot, z, 8:24], 0.0)
-                here_f = jnp.concatenate([edge, own], axis=0)
-                shift = 128 - 4 - 8 * j - 32 * ((i + 1) % 2)
-                side = pltpu.roll(halo, shift, 1)
-                sums = [None] * RANK
-                for t in range(TAPS):
-                    s = t - HALF
-                    if s == 0:
-                        moved = here_f
-                    elif s > 0:
-                        moved = pltpu.roll(jnp.where(lane24 < s, side, here_f), 128 - s, 1)
-                    else:
-                        moved = pltpu.roll(jnp.where(lane24 >= 128 + s, side, here_f), -s, 1)
-                    for r in range(RANK):
-                        term = kx[r][t] * moved
-                        sums[r] = term if sums[r] is None else sums[r] + term
-                for r in range(RANK):
-                    after_x[r, z] = sums[r]
-            return carry
-
-        lax.fori_loop(0, 4, x_step, 0)
-        kz = taps(view, 0, flipped)
+                lines = jnp.concatenate([edge_rows(slot, z, ok8), own], axis=0)
+
+                def store(r, value):
+                    after_x[r, z] = value
+
+                x_lines(lines, kx, store)
+            return carry
+
+        lax.fori_loop(0, 2, far_step, 0)
+        always = jnp.full((8, 128), 1, jnp.int32)
+
+        def near_step(i, carry):
+            for j in range(4):
+                z = 4 + i * 4 + j
+
+                def store(r, value):
+                    after_x[r, z, 0:8] = value
+
+                x_lines(edge_rows(slot, z, always), kx, store)
+            return carry
+
+        lax.fori_loop(0, 2, near_step, 0)
 
         def z_step(z, carry):
             for r in range(RANK):
@@ -214,18 +245,55 @@
             return carry
 
         lax.fori_loop(0, 8, z_step, 0)
-        ky = taps(view, 1, flipped)
-
-        def y_step(z, pack):
+
+        def y_step(z, carry):
+            part[z] = y_lines(ky, z)
+            return carry
+
+        lax.fori_loop(0, 8, y_step, 0)
+        wait_halos(slot, 1, recv_sem)
+        wait_halos(slot, 0, send_sem)
+        wait_halos(slot, 1, send_sem)
+
+        groups = []
+        for dz in range(3):
+            seen = []
+            for dy in range(3):
+                left, right = edge_in[slot, 0, dz, dy], edge_in[slot, 1, dz, dy]
+                seen.append(jnp.where((lane16 % 8) >= 4, right, left))
+            ok = (inside["gz"][0], 1, inside["gz"][1])[dz]
+            ok8 = jnp.logical_and(jnp.full((8, 128), ok, jnp.int32) > 0, cols_ok > 0)
+            edge = jnp.where(sub8 < 4, seen[2][0:8], seen[0][8:16])
+            edge = jnp.where(jnp.logical_and(rows_ok > 0, ok8), edge, 0.0)
+            rows = [edge] + [jnp.where(ok8, seen[1][8 * h : 8 * h + 8], 0.0) for h in range(2)]
+            groups.append(pltpu.roll(jnp.concatenate(rows, axis=0), (96, 32, 96)[dz], 1))
+        lines = jnp.where(lane24 < 32, groups[0], jnp.where(lane24 < 96, groups[1], groups[2]))
+        moved = [pltpu.roll(lines, (8 * (HALF - t)) % 128, 1) if t != HALF else lines for t in range(TAPS)]
+        spot24 = lane24 % 8
+        for r in range(RANK):
+            over_z = None
+            for t in range(TAPS):
+                term = kz[r][t] * moved[t]
+                over_z = term if over_z is None else over_z + term
             total = None
-            for r in range(RANK):
-                for t in range(TAPS):
-                    term = ky[r][t] * after_z[r, z, HALF + t : HALF + t + 16]
-                    total = term if total is None else total + term
-            plane = use(z, total)
-            return packed(pack, plane, z)
-
-        return lax.fori_loop(0, 8, y_step, jnp.zeros((16, 128), F32))
+            for d in range(HALF):
+                below = pltpu.roll(over_z, 128 - d, 1) if d else over_z
+                above = pltpu.roll(over_z, d, 1) if d else over_z
+                below = jnp.where(spot24 + d <= 3, below, 0.0)
+                above = jnp.where(spot24 - d >= 4, above, 0.0)
+                term = kx[r][d] * below + kx[r][TAPS - 1 - d] * above
+                total = term if total is None else total + term
+            after_z[r, 0, 0:24] = total
+            after_z[r, 0, 24:32] = total[0:8]
+        beyond = y_lines(ky, 0)
+        beyond = jnp.where((lane16 % 8) < 4, pltpu.roll(beyond, 124, 1), pltpu.roll(beyond, 4, 1))
+        at_edge = jnp.logical_or(lane16 < 4, lane16 >= 124)
+        pack = jnp.zeros((16, 128), F32)
+        for z in range(8):
+            add = pltpu.roll(beyond, 128 - (8 * (z + 4) + 4), 1)
+            plane = use(z, part[z] + jnp.where(at_edge, add, 0.0))
+            pack = packed(pack, plane, z)
+        return pack
 
     pack = jnp.zeros((16, 128), F32)
     for z in range(8):
@@ -236,28 +304,21 @@
 
     pl.semaphore_wait(barrier, len(AROUND))
 
-    for copy in halo_copies(0):
-        copy.start()
+    send_halos(0)
     for view in range(views):
         for copy in raw_copies(view):
             copy.start()
 
     def view_step(view, carry):
-        make_data(view)
         norm = norm_of(view)
-        for copy in halo_copies(0):
-            copy.wait()
 
         def to_ratio(z, total):
             plane = data[z] / (total * norm)
             field[1, 4 + z, 8:24] = plane
             return plane
 
-        edge_out[1] = blur(0, view, False, to_ratio)
-        for copy in halo_copies(1):
-            copy.start()
-        for copy in halo_copies(1):
-            copy.wait()
+        edge_out[1] = blur(0, view, False, to_ratio, lambda: make_data(view))
+        send_halos(1)
 
         def to_current(z, total):
             plane = field[0, 4 + z, 8:24] * (total * norm)
@@ -265,12 +326,11 @@
             out_ref[z] = plane
             return plane
 
-        edge_out[0] = blur(1, view, True, to_current)
+        edge_out[0] = blur(1, view, True, to_current, lambda: None)
 
         @pl.when(view < views - 1)
         def _():
-            for copy in halo_copies(0):
-                copy.start()
+            send_halos(0)
 
         return carry
 
@@ -283,7 +343,6 @@
     def shards(raw_views, interp_weight, sample_index, psf, estimate):
         vmem = pl.BlockSpec(memory_space=pltpu.VMEM)
         smem = pl.BlockSpec(memory_space=pltpu.SMEM)
-        num = len(AROUND)
         views = raw_views.shape[0]
 
         def body(*refs):
@@ -298,13 +357,13 @@
                 pltpu.VMEM((2, 16, 32, 128), F32),
                 pltpu.VMEM((2, 16, 128), F32),
                 pltpu.VMEM((2, 2, 3, 3, 16, 128), F32),
-                pltpu.VMEM((3, 24, 128), F32),
+                pltpu.VMEM((8, 16, 128), F32),
                 pltpu.VMEM((RANK, 16, 24, 128), F32),
                 pltpu.VMEM((RANK, 8, 32, 128), F32),
                 pltpu.VMEM((2, views, 8, 16, 128), F32),
                 pltpu.VMEM((8, 16, 128), F32),
-                pltpu.SemaphoreType.DMA((2, num)),
-                pltpu.SemaphoreType.DMA((2, num)),
+                pltpu.SemaphoreType.DMA((2, 2)),
+                pltpu.SemaphoreType.DMA((2, 2)),
                 pltpu.SemaphoreType.DMA((2, views)),
                 pltpu.SemaphoreType.DMA((2, views)),
             ],

time: 79.8 us -> 70.7 us (0.89)
  Pallas kernels: 78.2 us -> 69.1 us
    pallas_call x1, Pallas kernels: 78.2 us -> 69.1 us  [shards(): pl.pallas_call(body, out_shape=jax.ShapeDtypeStruct(estimate.shape, F32),...]
where the time goes in v3:
time: 70.7 us; the launch traced here: 70.6 us
  Pallas kernels  69.1 us (98%)
  local copies, waits for them, and re-layouts  1.47 us (2%)
    pallas_call x1, Pallas kernels, shards(): pl.pallas_call(body, out_shape=jax.ShapeDtypeStruct(estimate.shape, F32),...  69.1 us
    unnamed x1, local copies, waits for them, and re-layouts  1.47 us

profile of v3, /device:TPU:1, one launch (start us, length us, event | category | flops | bytes accessed | tf_op | source)
XLA Modules:
  0.0 70.6 jit_solution(2993998324338828774)
XLA Ops:
  0.0 69.1 %deconvolve.1 = f32[8,16,128]{2,1,0:T(8,128)} custom-call(f32[4,3,4,9]{3,2,1,0:T(4,128)} %refs_0_.1, f32[4,1024]{1,0:T(4,128)} %refs_1_.1, s32[4,1024]{1,0:T(4,128)} %refs_2_.1, f32[4,8,16,128]{3,2,1,0:T(8,128)} %refs_3_.1, f32[8,16,128]{2,1,0:T(8,128)} %refs_4_.1), custom_call_target="tpu_custom_call" | custom-call | tf_op jit(solution)/shard_map/deconvolve/pallas_call | solution.py:351
  69.1 1.5 %copy.7 = f32[8,16,128]{2,1,0:T(8,128)} copy(f32[8,16,128]{2,1,0:T(8,128)} %deconvolve.1) | data formatting | bytes 131072

commit v4 on v3

--- a/solution.py
+++ b/solution.py
@@ -9,6 +9,7 @@
 F32 = jnp.float32
 STEPS = (-1, 0, 1)
 AROUND = [(dz, dy, dx) for dx in STEPS for dz in STEPS for dy in STEPS if (dz, dy, dx) != (0, 0, 0)]
+AROUND.sort(key=lambda o: (o[2] != 0, -abs(o[0]) - abs(o[1])))
 HALF = 4
 TAPS = 9
 RANK = 4
@@ -244,13 +245,13 @@
                 after_z[r, z, 24:32] = total[0:8]
             return carry
 
-        lax.fori_loop(0, 8, z_step, 0)
+        lax.fori_loop(0, 8, z_step, 0, unroll=2)
 
         def y_step(z, carry):
             part[z] = y_lines(ky, z)
             return carry
 
-        lax.fori_loop(0, 8, y_step, 0)
+        lax.fori_loop(0, 8, y_step, 0, unroll=4)
         wait_halos(slot, 1, recv_sem)
         wait_halos(slot, 0, send_sem)
         wait_halos(slot, 1, send_sem)
@@ -305,9 +306,8 @@
     pl.semaphore_wait(barrier, len(AROUND))
 
     send_halos(0)
-    for view in range(views):
-        for copy in raw_copies(view):
-            copy.start()
+    for copy in raw_copies(0):
+        copy.start()
 
     def view_step(view, carry):
         norm = norm_of(view)
@@ -319,6 +319,11 @@
 
         edge_out[1] = blur(0, view, False, to_ratio, lambda: make_data(view))
         send_halos(1)
+
+        @pl.when(view < views - 1)
+        def _():
+            for copy in raw_copies(view + 1):
+                copy.start()
 
         def to_current(z, total):
             plane = field[0, 4 + z, 8:24] * (total * norm)

time: 70.7 us -> 67.3 us (0.952)
  Pallas kernels: 69.1 us -> 65.7 us
    pallas_call x1, Pallas kernels: 69.1 us -> 65.7 us  [shards(): pl.pallas_call(body, out_shape=jax.ShapeDtypeStruct(estimate.shape, F32),...]
where the time goes in v4:
time: 67.3 us; the launch traced here: 67.2 us
  Pallas kernels  65.7 us (98%)
  local copies, waits for them, and re-layouts  1.47 us (2%)
    pallas_call x1, Pallas kernels, shards(): pl.pallas_call(body, out_shape=jax.ShapeDtypeStruct(estimate.shape, F32),...  65.7 us
    unnamed x1, local copies, waits for them, and re-layouts  1.47 us

profile of v4, /device:TPU:1, one launch (start us, length us, event | category | flops | bytes accessed | tf_op | source)
XLA Modules:
  0.0 67.2 jit_solution(1469998150356587910)
XLA Ops:
  0.0 65.7 %deconvolve.1 = f32[8,16,128]{2,1,0:T(8,128)} custom-call(f32[4,3,4,9]{3,2,1,0:T(4,128)} %refs_0_.1, f32[4,1024]{1,0:T(4,128)} %refs_1_.1, s32[4,1024]{1,0:T(4,128)} %refs_2_.1, f32[4,8,16,128]{3,2,1,0:T(8,128)} %refs_3_.1, f32[8,16,128]{2,1,0:T(8,128)} %refs_4_.1), custom_call_target="tpu_custom_call" | custom-call | tf_op jit(solution)/shard_map/deconvolve/pallas_call | solution.py:356
  65.7 1.5 %copy.7 = f32[8,16,128]{2,1,0:T(8,128)} copy(f32[8,16,128]{2,1,0:T(8,128)} %deconvolve.1) | data formatting | bytes 131072

commit v5 on v4

--- a/solution.py
+++ b/solution.py
@@ -221,7 +221,7 @@
                 x_lines(lines, kx, store)
             return carry
 
-        lax.fori_loop(0, 2, far_step, 0)
+        lax.fori_loop(0, 2, far_step, 0, unroll=True)
         always = jnp.full((8, 128), 1, jnp.int32)
 
         def near_step(i, carry):
@@ -234,7 +234,7 @@
                 x_lines(edge_rows(slot, z, always), kx, store)
             return carry
 
-        lax.fori_loop(0, 2, near_step, 0)
+        lax.fori_loop(0, 2, near_step, 0, unroll=True)
 
         def z_step(z, carry):
             for r in range(RANK):

time: 67.3 us -> 66.4 us (0.987)
  Pallas kernels: 65.7 us -> 64.8 us
    pallas_call x1, Pallas kernels: 65.7 us -> 64.8 us  [shards(): pl.pallas_call(body, out_shape=jax.ShapeDtypeStruct(estimate.shape, F32),...]
where the time goes in v5:
time: 66.4 us; the launch traced here: 66.3 us
  Pallas kernels  64.8 us (98%)
  local copies, waits for them, and re-layouts  1.47 us (2%)
    pallas_call x1, Pallas kernels, shards(): pl.pallas_call(body, out_shape=jax.ShapeDtypeStruct(estimate.shape, F32),...  64.8 us
    unnamed x1, local copies, waits for them, and re-layouts  1.47 us

profile of v5, /device:TPU:1, one launch (start us, length us, event | category | flops | bytes accessed | tf_op | source)
XLA Modules:
  0.0 66.3 jit_solution(16246673708428487499)
XLA Ops:
  0.0 64.8 %deconvolve.1 = f32[8,16,128]{2,1,0:T(8,128)} custom-call(f32[4,3,4,9]{3,2,1,0:T(4,128)} %refs_0_.1, f32[4,1024]{1,0:T(4,128)} %refs_1_.1, s32[4,1024]{1,0:T(4,128)} %refs_2_.1, f32[4,8,16,128]{3,2,1,0:T(8,128)} %refs_3_.1, f32[8,16,128]{2,1,0:T(8,128)} %refs_4_.1), custom_call_target="tpu_custom_call" | custom-call | tf_op jit(solution)/shard_map/deconvolve/pallas_call | solution.py:356
  64.8 1.5 %copy.7 = f32[8,16,128]{2,1,0:T(8,128)} copy(f32[8,16,128]{2,1,0:T(8,128)} %deconvolve.1) | data formatting | bytes 131072

commit v6 on v5

--- a/solution.py
+++ b/solution.py
@@ -303,14 +303,15 @@
         pack = packed(pack, plane, z)
     edge_out[0] = pack
 
+    first_norm = norm_of(0)
     pl.semaphore_wait(barrier, len(AROUND))
 
     send_halos(0)
     for copy in raw_copies(0):
         copy.start()
 
-    def view_step(view, carry):
-        norm = norm_of(view)
+    def view_step(view, norm):
+        following = []
 
         def to_ratio(z, total):
             plane = data[z] / (total * norm)
@@ -331,15 +332,15 @@
             out_ref[z] = plane
             return plane
 
-        edge_out[0] = blur(1, view, True, to_current, lambda: None)
+        edge_out[0] = blur(1, view, True, to_current, lambda: following.append(norm_of(lax.min(view + 1, views - 1))))
 
         @pl.when(view < views - 1)
         def _():
             send_halos(0)
 
-        return carry
-
-    lax.fori_loop(0, views, view_step, 0)
+        return following[0]
+
+    lax.fori_loop(0, views, view_step, first_norm)
 
 
 def solution(mesh):

time: 66.4 us -> 66.3 us (level)
  no operation moved by 1% of the time
where the time goes in v6:
time: 66.3 us; the launch traced here: 66.1 us
  Pallas kernels  64.7 us (98%)
  local copies, waits for them, and re-layouts  1.47 us (2%)
    pallas_call x1, Pallas kernels, shards(): pl.pallas_call(body, out_shape=jax.ShapeDtypeStruct(estimate.shape, F32),...  64.7 us
    unnamed x1, local copies, waits for them, and re-layouts  1.47 us

profile of v6, /device:TPU:1, one launch (start us, length us, event | category | flops | bytes accessed | tf_op | source)
XLA Modules:
  0.0 66.1 jit_solution(8800810665814412512)
XLA Ops:
  0.0 64.7 %deconvolve.1 = f32[8,16,128]{2,1,0:T(8,128)} custom-call(f32[4,3,4,9]{3,2,1,0:T(4,128)} %refs_0_.1, f32[4,1024]{1,0:T(4,128)} %refs_1_.1, s32[4,1024]{1,0:T(4,128)} %refs_2_.1, f32[4,8,16,128]{3,2,1,0:T(8,128)} %refs_3_.1, f32[8,16,128]{2,1,0:T(8,128)} %refs_4_.1), custom_call_target="tpu_custom_call" | custom-call | tf_op jit(solution)/shard_map/deconvolve/pallas_call | solution.py:357
  64.7 1.5 %copy.7 = f32[8,16,128]{2,1,0:T(8,128)} copy(f32[8,16,128]{2,1,0:T(8,128)} %deconvolve.1) | data formatting | bytes 131072
